TPU v7x, 512 devices: a whole 4x8x8 slice. The times are simulated.
512 devices in a mesh: row: 32 (over x, y_lo, core), col: 16 (over y_hi, z).
Axes of the slice: x: 4, y: 8 (y_hi: 2, y_lo: 4; y = y_hi * 4 + y_lo), z: 8, core: 2. Of those that a mesh axis runs over, the one named last changes fastest.
Arguments:
- tile_entries: float32 [32, 16, 64, 128, 128], P('row', 'col'), may hold values from 0 to 65520, as said below
- tile_rows: int32 [32, 16, 64], P('row', 'col'), may hold values from 0 to 31, as said below
- tile_cols: int32 [32, 16, 64], P('row', 'col'), may hold values from 0 to 63, as said below
- tile_count: int32 [32, 16], P('row', 'col'), may hold values from 8 to 64, as said below
- block_x: float32 [64, 131072], P(None, ('row', 'col')), may hold values from 0 to 65520, as said below
- block_y: float32 [64, 131072], P(None, ('row', 'col')), may hold values from 0 to 65520, as said below
Outputs:
- matrix_poly: float32 [3, 64, 64], replicated
- vector_last: float32 [64, 131072], P(None, ('row', 'col'))
Inputs may be any that keep to these rules, and one draw needn't show every extreme that they name: `tile_entries`: whole numbers. `block_x`: whole numbers. `block_y`: whole numbers. The slots of one device name distinct block pairs (tile_rows, tile_cols), among them (0, 0) and (31, 63) in some slot. `tile_cols`: block column k of column group c is the global block column (k // 2) * 32 + c * 2 + k % 2. Slots 0 to tile_count - 1 of a device hold its tiles, the rest are unused; some device fills all 64 slots.
All inputs are finite; a program needn't handle non-finite values.
Results may differ from a plain program's by a relative error of at most 0.0003.
Values sent between devices are 32-bit elements; how exact they have to be, the bound alone decides.
A program may use at most 64 MiB of HBM per device.

v0:
```python
import jax
import jax.numpy as jnp
from jax import lax
from jax.sharding import PartitionSpec as P

STEP_COUNT = 3


MODULUS = 65521.0
HALF_MODULUS = 32760.0


def reduce_mod(values):
    quotient = jnp.floor(values / MODULUS)
    leftover = values - quotient * MODULUS
    leftover = jnp.where(leftover < 0, leftover + MODULUS, leftover)
    return jnp.where(leftover >= MODULUS, leftover - MODULUS, leftover)


def split_digits(values):
    high_digit = jnp.floor(values / 256.0)
    return (high_digit, values - 256.0 * high_digit)


def combine_parts(high_part, middle_part, low_part):
    return reduce_mod(
        15.0 * reduce_mod(high_part)
        + reduce_mod(256.0 * reduce_mod(middle_part))
        + reduce_mod(low_part)
    )


def centered(residues):
    return jnp.where(residues > HALF_MODULUS, residues - MODULUS, residues)


def vector_digits(vector):
    high_v, low_v = split_digits(vector)
    return jnp.concatenate([high_v, low_v], 0).astype(jnp.bfloat16)


def poly_product(left_side, right_side):
    span_width = left_side.shape[-1]
    left_high, left_low = split_digits(left_side)
    right_high, right_low = split_digits(right_side)
    stacked_left = jnp.concatenate([left_high, left_low], 1).astype(jnp.bfloat16)
    stacked_right = jnp.concatenate([right_high, right_low], 2).astype(jnp.bfloat16)
    products = jnp.einsum(
        "kmj,kjn->kmn", stacked_left, stacked_right, preferred_element_type=jnp.float32
    )
    return combine_parts(
        products[:, :span_width, :span_width],
        products[:, :span_width, span_width:] + products[:, span_width:, :span_width],
        products[:, span_width:, span_width:],
    )


def sigma_update(projections):
    span_width = projections[0].shape[0]
    term_count = len(projections) + 1
    identity = jnp.eye(span_width, dtype=jnp.float32)[None]
    polynomial = jnp.concatenate(
        [identity, jnp.zeros((term_count - 1, span_width, span_width), jnp.float32)], 0
    )
    for step_index in range(1, term_count):
        known_terms = jnp.stack(
            [projections[step_index - 1 - shift] for shift in range(step_index)]
        )
        discrepancy = reduce_mod(jnp.sum(poly_product(polynomial[:step_index], known_terms), 0))
        scaled = poly_product(jnp.broadcast_to(discrepancy, polynomial.shape), polynomial)
        shifted = jnp.concatenate(
            [jnp.zeros((1, span_width, span_width), jnp.float32), polynomial[:-1]], 0
        )
        polynomial = reduce_mod(shifted - scaled)
    return polynomial


def project_local(x_part, v_part, tile_len):
    span_width = x_part.shape[0]
    block_total = x_part.shape[1] // tile_len
    x_digits = vector_digits(x_part).reshape(2 * span_width, block_total, tile_len)
    v_digits = vector_digits(v_part).reshape(2 * span_width, block_total, tile_len)
    products = jnp.einsum("mbk,nbk->bmn", x_digits, v_digits, preferred_element_type=jnp.float32)
    residues = combine_parts(
        products[:, :span_width, :span_width],
        products[:, :span_width, span_width:] + products[:, span_width:, :span_width],
        products[:, span_width:, span_width:],
    )
    return reduce_mod(jnp.sum(residues, 0))


def local(tile_entries, tile_rows, tile_cols, tile_count, block_x, block_y):
    entries = tile_entries[0, 0]
    rows_here = tile_rows[0, 0]
    cols_here = tile_cols[0, 0]
    count_here = tile_count[0, 0]
    slot_count = entries.shape[0]
    tile_len = entries.shape[1]
    span_width = block_y.shape[0]
    piece_len = block_y.shape[1]
    row_blocks = piece_len // tile_len * lax.axis_size("col")
    high_a, low_a = split_digits(entries)
    a_digits = jnp.stack([high_a, low_a], 1).astype(jnp.bfloat16)
    live_slots = (jnp.arange(slot_count, dtype=jnp.int32) < count_here).astype(jnp.float32)
    onehot = (rows_here[None, :] == jnp.arange(row_blocks, dtype=jnp.int32)[:, None]).astype(
        jnp.float32
    )
    onehot = onehot * live_slots[None, :]
    vector = block_y
    projections = []
    for step_index in range(STEP_COUNT):
        gathered = lax.all_gather(vector, "row", axis=1, tiled=True)
        v_digits = vector_digits(gathered).reshape(2 * span_width, -1, tile_len)
        picked = jnp.take(v_digits, cols_here, axis=1)
        products = jnp.einsum(
            "ntk,tdik->tdni", picked, a_digits, preferred_element_type=jnp.float32
        )
        residues = combine_parts(
            products[:, 0, :span_width],
            products[:, 0, span_width:] + products[:, 1, :span_width],
            products[:, 1, span_width:],
        )
        summed = jnp.einsum("bt,twi->wbi", onehot, residues, precision=lax.Precision.HIGHEST)
        partial_rows = reduce_mod(summed).reshape(span_width, row_blocks * tile_len)
        whole_sum = lax.psum(partial_rows, "col")
        reduced = lax.dynamic_slice_in_dim(
            whole_sum, lax.axis_index("col") * piece_len, piece_len, 1
        )
        vector = reduce_mod(reduced)
        partial_terms = centered(project_local(block_x, vector, tile_len))
        projections.append(reduce_mod(lax.psum(partial_terms, ("row", "col"))))
    polynomial = sigma_update(projections)
    return (polynomial[:-1] / MODULUS, vector / MODULUS)


def solution(mesh):
    placed = (
        P("row", "col", None, None, None),
        P("row", "col", None),
        P("row", "col", None),
        P("row", "col"),
        P(None, ("row", "col")),
        P(None, ("row", "col")),
    )
    return jax.shard_map(
        local, mesh=mesh, in_specs=placed, out_specs=(P(), P(None, ("row", "col"))), check_vma=False
    )
```

profile of v0, /device:TPU:1, one launch (start us, length us, event | category | flops | bytes accessed | tf_op | source)
XLA Modules:
  0.0 971.5 jit_solution(7593107498420893657)
XLA Ops:
  7.2 0.7 all-gather.4.cloned.1.call-update
  8.6 0.7 compare_select_fusion.159
  9.3 0.7 compare_and_fusion
  9.9 4.8 fusion.2
  14.7 63.7 %all-gather.4.cloned.1.call-done = f32[64,8192]{1,0:T(8,128)} async-done(((f32[64,256]{1,0:T(8,128)}), f32[64,8192]{1,0:T(8,128)}) %all-gather.4.cloned.1.call-update) | async-done | bytes 2097168 | tf_op jit(solution)/shard_map/all_gather | solution.py:112
  78.4 2.1 fusion.53
  80.5 0.6 copy_bitcast_fusion.7
  81.1 1.5 pad_maximum_fusion.1
  82.6 3.8 gather_fusion
  86.3 3.5 convolution_bitcast_fusion
  89.9 3.8 compare_select_fusion.20
  93.7 2.7 compare_select_fusion.34
  96.5 1.6 copy.149
  98.1 188.7 %all-reduce.9.cloned.1.call-done = f32[64,4096]{1,0:T(8,128)} async-done(((f32[64,4096]{1,0:T(8,128)}), f32[64,4096]{1,0:T(8,128)}) %all-reduce.9.cloned.1.call-update) | async-done | bytes 1048592 | tf_op jit(solution)/shard_map/psum | solution.py:125
  286.8 1.5 fusion.162
  288.6 71.6 %all-gather.6.cloned.1.call-done = f32[64,8192]{1,0:T(8,128)} async-done(((f32[64,256]{1,0:T(8,128)}), f32[64,8192]{1,0:T(8,128)}) %all-gather.6.cloned.1.call-update) | async-done | bytes 2097168 | tf_op jit(solution)/shard_map/all_gather | solution.py:112
  360.2 2.1 fusion.55
  362.3 0.3 copy.152
  362.6 0.3 copy.153
  362.9 1.5 pad_maximum_fusion.2
  364.4 3.8 gather_fusion.1
  368.1 3.5 fusion.7
  371.7 3.8 compare_select_fusion.10
  375.5 2.7 compare_select_fusion.32
  378.3 1.6 copy.148
  379.9 188.9 %all-reduce.11.cloned.1.call-done = f32[64,4096]{1,0:T(8,128)} async-done(((f32[64,4096]{1,0:T(8,128)}), f32[64,4096]{1,0:T(8,128)}) %all-reduce.11.cloned.1.call-update) | async-done | bytes 1048592 | tf_op jit(solution)/shard_map/psum | solution.py:125
  568.8 1.5 fusion.164
  570.3 0.3 all-reduce.13.cloned.1.call-start
  570.9 71.0 %all-gather.8.cloned.1.call-done = f32[64,8192]{1,0:T(8,128)} async-done(((f32[64,256]{1,0:T(8,128)}), f32[64,8192]{1,0:T(8,128)}) %all-gather.8.cloned.1.call-update) | async-done | bytes 2097168 | tf_op jit(solution)/shard_map/all_gather | solution.py:112
  642.0 2.1 fusion.57
  644.1 0.3 copy.150
  644.4 0.3 copy.151
  644.7 1.5 pad_maximum_fusion.3
  646.2 3.7 gather_fusion.2
  649.9 3.5 fusion.10
  653.4 3.8 compare_select_fusion
  657.3 2.7 compare_select_fusion.30
  660.0 1.6 copy.147
  662.3 188.2 %all-reduce.13.cloned.1.call-done = f32[64,4096]{1,0:T(8,128)} async-done(((f32[64,4096]{1,0:T(8,128)}), f32[64,4096]{1,0:T(8,128)}) %all-reduce.13.cloned.1.call-update) | async-done | bytes 1048592 | tf_op jit(solution)/shard_map/psum | solution.py:125
  850.5 1.5 broadcast_multiply_fusion
  852.4 107.2 %all-reduce.4 = (f32[64,64]{1,0:T(8,128)S(1)}, f32[64,64]{1,0:T(8,128)S(1)}, f32[64,64]{1,0:T(8,128)S(1)}) all-reduce(f32[64,64]{1,0:T(8,128)S(1)} %compare_select_fusion.156, f32[64,64]{1,0:T(8,128)S(1)} %compare_select_fusion.139, f32[64,64]{1,0:T(8,128)S(1)} %compare_select_fusion.132), channel_id=1, replica_groups=mesh['row'=32,'col'=16] {'row','col'}, use_global_device_ids=true, to_apply=%region_2.4 | all-reduce | flops 12288 | bytes 98304 | tf_op jit(solution)/shard_map/psum | solution.py:131
  960.2 0.3 fusion.118
  960.6 0.4 fusion.86
  961.8 0.3 fusion.133
  962.1 0.4 fusion.85
  963.3 0.3 fusion.144
  963.7 0.3 multiply_floor_fusion.3
  964.0 0.7 fusion.91
  (77 shorter events, 3.9 us)
Async XLA Ops:
  7.2 71.2 %all-gather.4.cloned.1.call-start = ((), (), s32[]{:S(2)}) async-start(), calls=%async_computation | async-start | bytes 2162688 | tf_op jit(solution)/shard_map/all_gather | solution.py:112
  7.9 278.9 %all-reduce.9.cloned.1.call-start = ((), (), s32[]{:S(2)}) async-start(), calls=%async_computation.1 | async-start | bytes 2097152 | tf_op jit(solution)/shard_map/psum | solution.py:125
  89.9 3.8 copy-start.4
  98.1 262.1 %all-gather.6.cloned.1.call-start = ((), (), s32[]{:S(2)}) async-start(), calls=%async_computation.2 | async-start | bytes 2162688 | tf_op jit(solution)/shard_map/all_gather | solution.py:112
  288.4 280.4 %all-reduce.11.cloned.1.call-start = ((), (), s32[]{:S(2)}) async-start(), calls=%async_computation.3 | async-start | bytes 2097152 | tf_op jit(solution)/shard_map/psum | solution.py:125
  378.2 192.4 %copy-start.3 = (f32[64,256]{1,0:T(8,128)S(1)}, f32[64,256]{1,0:T(8,128)}, u32[]{:S(2)}) copy-start(f32[64,256]{1,0:T(8,128)} %param.12) | copy-start | bytes 196612
  378.2 192.5 %copy-start = (f32[64,256]{1,0:T(8,128)S(1)}, f32[64,256]{1,0:T(8,128)}, u32[]{:S(2)}) copy-start(f32[64,256]{1,0:T(8,128)} %get-tuple-element.17) | copy-start | bytes 196612
  379.9 262.1 %all-gather.8.cloned.1.call-start = ((), (), s32[]{:S(2)}) async-start(), calls=%async_computation.4 | async-start | bytes 2162688 | tf_op jit(solution)/shard_map/all_gather | solution.py:112
  570.3 280.2 %all-reduce.13.cloned.1.call-start = ((), (), s32[]{:S(2)}) async-start(), calls=%async_computation.5 | async-start | bytes 2097152 | tf_op jit(solution)/shard_map/psum | solution.py:125
  570.6 73.4 %copy-start.2 = (f32[4,64,64]{2,1,0:T(8,128)}, f32[4,64,64]{2,1,0:T(8,128)S(1)}, u32[]{:S(2)}) copy-start(f32[4,64,64]{2,1,0:T(8,128)S(1)} %pad_convert_fusion) | copy-start | bytes 196612
  660.0 1.9 copy-start.1
  661.6 298.9 %slice-start = ((f32[4,64,64]{2,1,0:T(8,128)}), f32[3,64,64]{2,1,0:T(8,128)S(1)}, s32[]{:S(2)}) async-start(f32[4,64,64]{2,1,0:T(8,128)} %copy-done.2), calls=%async_computation.6 | async-start | bytes 196608 | tf_op jit(solution)/shard_map/slice | solution.py:72
Sparse Core Ops, SparseCore 0:
  10.1 68.1 all-gather.3
  98.2 188.6 all-reduce.8
  289.6 70.5 all-gather.5
  380.0 188.7 all-reduce.10
  571.4 70.5 all-gather.7
  661.8 188.6 all-reduce.12
where the time goes:
time: 972 us
  waiting for transfers between devices  773 us (80%)
  blocking collectives  107 us (11%)
  other arithmetic  36.2 us (4%)
  matrix products  20.9 us (2%)
  local copies, waits for them, and re-layouts  18.4 us (2%)
  between operations  15.3 us (2%)
    psum x3, waiting for transfers between devices, local(): whole_sum = lax.psum(partial_rows, 'col')  566 us
    all_gather x3, waiting for transfers between devices, local(): gathered = lax.all_gather(vector, 'row', axis=1, tiled=True)  206 us
    psum x1, blocking collectives, local(): projections.append(reduce_mod(lax.psum(partial_terms, ('row', 'col'))))  107 us
  transfers between devices with their start and end apart: 6, of which 6 were waited for; matrix products, arithmetic and copies ran while one was open for 1% of the time, Pallas kernels for 0%

commit v1 on v0

v1 whole, which is shorter than its diff:
```python
import functools

import jax
import jax.numpy as jnp
from jax import lax
from jax.experimental import pallas as pl
from jax.experimental.pallas import tpu as pltpu
from jax.sharding import PartitionSpec as P

STEP_COUNT = 3
MODULUS = 65521.0
INVERSE = 1.0 / 65521.0
MESH = pl.DeviceIdType.MESH
NX, NYL, NYH, NZ = 4, 4, 2, 8
F32, I32, BF16 = jnp.float32, jnp.int32, jnp.bfloat16


def reduce_mod(values):
    leftover = values - jnp.floor(values * INVERSE) * MODULUS
    leftover = jnp.where(leftover < 0, leftover + MODULUS, leftover)
    return jnp.where(leftover >= MODULUS, leftover - MODULUS, leftover)


def split_digits(values):
    high_digit = jnp.floor(values * (1.0 / 256.0))
    return (high_digit, values - 256.0 * high_digit)


def fold(values):
    high = values >> 16
    return (high << 4) - high + (values & 65535)


def times15(values):
    return (values << 4) - values


def kernel(
    order_ref, last_ref, entries_ref, x_ref, y_ref, c_ref, v_ref,
    ent, adig, xdig, gat, vdig, prods, part, lbuf, sbuf, ybuf, ysrc, vbuf, cloc, chalf, crecv, axb, ayb, azb,
    ent_sem, ys, yr, xs, xr, rs, rr, bs, br, ls, lr, hs, hr, ps, pr, cs, cr, axs, axr, ays, ayr, azs, azr,
):
    row, col = lax.axis_index("row"), lax.axis_index("col")
    core, yl, px = row % 2, (row // 2) % NYL, row // (2 * NYL)
    yh, pz = col // NZ, col % NZ
    step_r = 1 - 2 * core

    def rid(ax, ay, ac):
        return (((ax + 2 * NX) % NX) * NYL + (ay + 2 * NYL) % NYL) * 2 + ac

    def dev_x(d):
        return (rid(px + d, yl, core), col)

    def dev_y(d):
        whole = (yh * NYL + yl + d) % (NYL * NYH)
        return (rid(px, whole % NYL, core), (whole // NYL) * NZ + pz)

    def dev_z(d):
        return (row, yh * NZ + (pz + d + 2 * NZ) % NZ)

    sibling = (rid(px, yl, 1 - core), col)

    def remote(src, dst, ssem, rsem, dev):
        return pltpu.make_async_remote_copy(
            src_ref=src, dst_ref=dst, send_sem=ssem, recv_sem=rsem, device_id=dev, device_id_type=MESH
        )

    tile_total = ent.shape[0]
    chunk = 8

    def entry_copy(n):
        where = pl.ds(n * chunk, chunk)
        return pltpu.make_async_copy(entries_ref.at[where], ent.at[where], ent_sem.at[n])

    for n in range(tile_total // chunk):
        entry_copy(n).start()

    barrier = pltpu.get_barrier_semaphore()
    partners = [dev_x(d) for d in range(1, NX)] + [dev_y(d) for d in range(1, 8)]
    partners += [dev_z(d) for d in range(1, NZ)] + [sibling]
    for partner in partners:
        pl.semaphore_signal(barrier, inc=1, device_id=partner, device_id_type=MESH)

    high_x, low_x = split_digits(x_ref[...])
    xdig[0:64, :] = high_x.astype(BF16)
    xdig[64:128, :] = low_x.astype(BF16)
    vbuf[0] = y_ref[...]
    pl.semaphore_wait(barrier, len(partners))

    def gather(i, between):
        own = vbuf.at[i]
        sends = []

        def send(src, dst, ssem, rsem, dev):
            copy = remote(src, dst, ssem, rsem, dev)
            copy.start()
            sends.append(copy)

        def piece(r):
            return gat.at[i, r]

        def arrive(r, rsem):
            remote(piece(r), piece(r), bs.at[i, 0], rsem, sibling).wait_recv()

        def both_x(src, r, d):
            send(src, piece(r), xs.at[i, d, 0], xr.at[i, d, 0], dev_x(1))
            send(src, piece(r), xs.at[i, d, 1], xr.at[i, d, 1], dev_x(-1))

        def to_sibling(src, r, n):
            send(src, piece(r), bs.at[i, n], br.at[i, n], sibling)

        for d in range(1, NYL):
            target = (rid(px, yl + d, core), col)
            send(own, piece(row), ys.at[i, d - 1], yr.at[i, d - 1], target)
        both_x(own, row, 0)
        to_sibling(own, row, 0)
        gat[i, row] = vbuf[i]
        between(0)

        def relay(d):
            near = rid(px - step_r, yl - d, core)
            arrive(near, xr.at[i, d, core])
            send(piece(near), piece(near), rs.at[i, d], rr.at[i, d], dev_x(step_r))
            to_sibling(piece(near), near, 4 + d)

        for d in range(1, NYL):
            r = rid(px, yl - d, core)
            arrive(r, yr.at[i, d - 1])
            both_x(piece(r), r, d)
            to_sibling(piece(r), r, d)
            relay(d - 1)
            between(d)
        relay(NYL - 1)
        for d in range(NYL):
            other = rid(px + step_r, yl - d, core)
            arrive(other, xr.at[i, d, 1 - core])
            to_sibling(piece(other), other, 8 + d)
            far = rid(px + 2, yl - d, core)
            arrive(far, rr.at[i, d])
            to_sibling(piece(far), far, 12 + d)
        for n in range(16):
            shift = (0, step_r, -step_r, 2)[n // 4]
            arrive(rid(px + shift, yl - n % 4, 1 - core), br.at[i, n])
        for copy in sends:
            copy.wait_send()

    def make_digits(n):
        @pl.loop(n * chunk, (n + 1) * chunk)
        def _(t):
            high, low = split_digits(ent[t].T)
            adig[t, 0:128, :] = high.astype(BF16)
            adig[t, 128:256, :] = low.astype(BF16)

    def nothing(stage):
        del stage

    def first_between(stage):
        for n in (2 * stage, 2 * stage + 1):
            entry_copy(n).wait()
            make_digits(n)

    def multiply(i):
        @pl.loop(0, 32)
        def _(r):
            high, low = split_digits(gat[i, r])
            for j in range(2):
                vdig[2 * r + j, 0:64, :] = high[:, j * 128 : (j + 1) * 128].astype(BF16)
                vdig[2 * r + j, 64:128, :] = low[:, j * 128 : (j + 1) * 128].astype(BF16)

        blank = jnp.zeros((64, 128), BF16)
        width = 4

        def body(n, total):
            for u in range(width):
                j = n * width + u
                digits = vdig[order_ref[1, j]]
                high, low = digits[0:64], digits[64:128]
                left = jnp.concatenate(
                    [
                        jnp.concatenate([low, high], 1),
                        jnp.concatenate([high, blank], 1),
                        jnp.concatenate([blank, low], 1),
                    ],
                    0,
                )
                product = jnp.dot(left, adig[order_ref[0, j]], preferred_element_type=F32)
                total = (total & order_ref[2, j]) + product.astype(I32)
                prods[j] = total
            return total

        lax.fori_loop(0, tile_total // width, body, jnp.zeros((192, 128), I32))

    def slot_of(z, q):
        return (yh if q else 1 - yh) * NZ + (z + 2 * NZ) % NZ

    def fill(slot):
        for j in range(2):
            b = 2 * slot + j
            sums = prods[last_ref[0, b]] & last_ref[1, b]
            total = times15(fold(sums[64:128])) + (fold(sums[0:64]) << 8) + sums[128:192]
            part[slot, :, j * 128 : (j + 1) * 128] = reduce_mod(fold(total).astype(F32))

    def reduce(i):
        sends = []

        def long_copy(src, k, q):
            return remote(src, lbuf.at[i, k, q], ls.at[i, k, q], lr.at[i, k, q], dev_z(step_r))

        def short_copy(src, k, q):
            return remote(src, sbuf.at[i, k, q], hs.at[i, k, q], hr.at[i, k, q], dev_z(-step_r))

        def start(copy):
            copy.start()
            sends.append(copy)

        for q in range(2):
            slot = slot_of(pz + 4, q)
            fill(slot)
            start(long_copy(part.at[slot], 0, q))
            slot = slot_of(pz - 3 * step_r, q)
            fill(slot)
            start(short_copy(part.at[slot], 0, q))
        for k in range(3):
            for q in range(2):
                slot = slot_of(pz + (3 - k) * step_r, q)
                fill(slot)
                long_copy(part.at[slot], k, q).wait_recv()
                lbuf[i, k, q] = lbuf[i, k, q] + part[slot]
                start(long_copy(lbuf.at[i, k, q], k + 1, q))
                if k < 2:
                    slot = slot_of(pz - (2 - k) * step_r, q)
                    fill(slot)
                    short_copy(part.at[slot], k, q).wait_recv()
                    sbuf[i, k, q] = sbuf[i, k, q] + part[slot]
                    start(short_copy(sbuf.at[i, k, q], k + 1, q))
        swap = remote(ysrc.at[i], ybuf.at[i], ps.at[i], pr.at[i], dev_y(4))
        for q in range(2):
            slot = slot_of(pz, q)
            fill(slot)
            short_copy(part.at[slot], 2, q).wait_recv()
            long_copy(part.at[slot], 3, q).wait_recv()
            whole = lbuf[i, 3, q] + sbuf[i, 2, q] + part[slot]
            if q == 0:
                ysrc[i] = whole
                swap.start()
        swap.wait_recv()
        vbuf[i + 1] = reduce_mod(whole + ybuf[i])
        for copy in sends:
            copy.wait_send()
        swap.wait_send()

    def project(i):
        high, low = split_digits(vbuf[i + 1])
        digits = jnp.concatenate([high.astype(BF16), low.astype(BF16)], 0)
        products = lax.dot_general(
            xdig[...], digits, (((1,), (1,)), ((), ())), preferred_element_type=F32
        ).astype(I32)
        upper, lower = products[0:64], pltpu.roll(products[64:128], 64, 1)
        left_half = lax.broadcasted_iota(I32, (64, 128), 1) < 64
        mixed = jnp.where(left_half, times15(fold(upper)) + lower, fold(upper + lower) << 8)
        residues = reduce_mod(fold(mixed + pltpu.roll(mixed, 64, 1)).astype(F32))
        cloc[i] = jnp.where(left_half[0:32], residues[0:32], residues[32:64])

    gather(0, first_between)
    multiply(0)
    reduce(0)
    project(0)

    def later(i, carry):
        gather(i, nothing)
        multiply(i)
        reduce(i)
        project(i)
        return carry

    lax.fori_loop(1, STEP_COUNT, later, 0)
    v_ref[...] = vbuf[STEP_COUNT]

    halves = [remote(cloc.at[:, pl.ds(16 * (1 - core), 16)], crecv, cs.at[0], cr.at[0], sibling)]
    halves[0].start()
    halves[0].wait_recv()
    chalf[0] = cloc[:, pl.ds(16 * core, 16)] + crecv[...]

    def exchange(k, count, landing, ssem, rsem, dev):
        copies = []
        for d in range(1, count):
            copies.append(remote(chalf.at[k], landing.at[d - 1], ssem.at[d - 1], rsem.at[d - 1], dev(d)))
            copies[-1].start()
        total = chalf[k]
        for d in range(1, count):
            copies[d - 1].wait_recv()
            total = total + landing[d - 1]
        chalf[k + 1] = total if k == 0 else reduce_mod(total)
        halves.extend(copies)

    exchange(0, NX, axb, axs, axr, dev_x)
    exchange(1, NYL * NYH, ayb, ays, ayr, dev_y)
    exchange(2, NZ, azb, azs, azr, dev_z)
    mine = pl.ds(16 * core, 16)
    swap = remote(chalf.at[3], c_ref.at[:, mine], cs.at[1], cr.at[1], sibling)
    swap.start()
    c_ref[:, mine] = chalf[3]
    swap.wait_recv()
    swap.wait_send()
    for copy in halves:
        copy.wait_send()


def combine_parts(high_part, middle_part, low_part):
    return reduce_mod(
        15.0 * reduce_mod(high_part)
        + reduce_mod(256.0 * reduce_mod(middle_part))
        + reduce_mod(low_part)
    )


def poly_product(left_side, right_side):
    span_width = left_side.shape[-1]
    left_high, left_low = split_digits(left_side)
    right_high, right_low = split_digits(right_side)
    stacked_left = jnp.concatenate([left_high, left_low], 1).astype(BF16)
    stacked_right = jnp.concatenate([right_high, right_low], 2).astype(BF16)
    products = jnp.einsum("kmj,kjn->kmn", stacked_left, stacked_right, preferred_element_type=F32)
    return combine_parts(
        products[:, :span_width, :span_width],
        products[:, :span_width, span_width:] + products[:, span_width:, :span_width],
        products[:, span_width:, span_width:],
    )


def sigma_update(projections):
    span_width = projections[0].shape[0]
    term_count = len(projections) + 1
    identity = jnp.eye(span_width, dtype=F32)[None]
    polynomial = jnp.concatenate(
        [identity, jnp.zeros((term_count - 1, span_width, span_width), F32)], 0
    )
    for step_index in range(1, term_count):
        known_terms = jnp.stack(
            [projections[step_index - 1 - shift] for shift in range(step_index)]
        )
        discrepancy = reduce_mod(jnp.sum(poly_product(polynomial[:step_index], known_terms), 0))
        scaled = poly_product(jnp.broadcast_to(discrepancy, polynomial.shape), polynomial)
        shifted = jnp.concatenate(
            [jnp.zeros((1, span_width, span_width), F32), polynomial[:-1]], 0
        )
        polynomial = reduce_mod(shifted - scaled)
    return polynomial


def local(tile_entries, tile_rows, tile_cols, tile_count, block_x, block_y):
    entries = tile_entries[0, 0]
    slots = entries.shape[0]
    index = jnp.arange(slots, dtype=I32)
    keys = jnp.where(index < tile_count[0, 0], tile_rows[0, 0], 32)
    before = (keys[None, :] < keys[:, None]) | ((keys[None, :] == keys[:, None]) & (index[None, :] < index[:, None]))
    rank = jnp.sum(before.astype(I32), 1)
    chosen = (rank[None, :] == index[:, None]).astype(I32)
    order = jnp.sum(chosen * index[None, :], 1)
    columns = jnp.sum(chosen * tile_cols[0, 0][None, :], 1)
    sorted_keys = jnp.sum(chosen * keys[None, :], 1)
    same = jnp.concatenate([jnp.zeros((1,), jnp.bool_), sorted_keys[1:] == sorted_keys[:-1]])
    order_table = jnp.stack([order, columns, -same.astype(I32)])
    blocks = jnp.arange(32, dtype=I32)
    below = jnp.sum((keys[None, :] <= blocks[:, None]).astype(I32), 1)
    found = jnp.any(keys[None, :] == blocks[:, None], 1)
    last_table = jnp.stack([jnp.maximum(below - 1, 0), -found.astype(I32)])

    vmem = pl.BlockSpec(memory_space=pltpu.VMEM)
    smem = pl.BlockSpec(memory_space=pltpu.SMEM)
    steps = STEP_COUNT
    dma = pltpu.SemaphoreType.DMA
    projections, vector = pl.pallas_call(
        kernel,
        out_shape=(
            jax.ShapeDtypeStruct((steps, 32, 128), F32),
            jax.ShapeDtypeStruct((64, 256), F32),
        ),
        in_specs=[smem, smem, pl.BlockSpec(memory_space=pl.ANY), vmem, vmem],
        out_specs=(vmem, vmem),
        scratch_shapes=[
            pltpu.VMEM((slots, 128, 128), F32),
            pltpu.VMEM((slots, 256, 128), BF16),
            pltpu.VMEM((128, 256), BF16),
            pltpu.VMEM((steps, 32, 64, 256), F32),
            pltpu.VMEM((64, 128, 128), BF16),
            pltpu.VMEM((slots, 192, 128), I32),
            pltpu.VMEM((16, 64, 256), F32),
            pltpu.VMEM((steps, 4, 2, 64, 256), F32),
            pltpu.VMEM((steps, 3, 2, 64, 256), F32),
            pltpu.VMEM((steps, 64, 256), F32),
            pltpu.VMEM((steps, 64, 256), F32),
            pltpu.VMEM((steps + 1, 64, 256), F32),
            pltpu.VMEM((steps, 32, 128), F32),
            pltpu.VMEM((4, steps, 16, 128), F32),
            pltpu.VMEM((steps, 16, 128), F32),
            pltpu.VMEM((NX - 1, steps, 16, 128), F32),
            pltpu.VMEM((7, steps, 16, 128), F32),
            pltpu.VMEM((7, steps, 16, 128), F32),
            dma((8,)),
            dma((steps, 3)), dma((steps, 3)),
            dma((steps, 4, 2)), dma((steps, 4, 2)),
            dma((steps, 4)), dma((steps, 4)),
            dma((steps, 16)), dma((steps, 16)),
            dma((steps, 4, 2)), dma((steps, 4, 2)),
            dma((steps, 3, 2)), dma((steps, 3, 2)),
            dma((steps,)), dma((steps,)),
            dma((2,)), dma((2,)),
            dma((3,)), dma((3,)),
            dma((7,)), dma((7,)),
            dma((7,)), dma((7,)),
        ],
        compiler_params=pltpu.CompilerParams(
            collective_id=0, has_side_effects=True, vmem_limit_bytes=56 * 1024 * 1024
        ),
    )(order_table, last_table, entries, block_x, block_y)
    projections = jnp.concatenate([projections[:, :, :64], projections[:, :, 64:]], 1)
    polynomial = sigma_update([projections[n] for n in range(steps)])
    return (polynomial[:-1] / MODULUS, vector / MODULUS)


def solution(mesh):
    placed = (
        P("row", "col", None, None, None),
        P("row", "col", None),
        P("row", "col", None),
        P("row", "col"),
        P(None, ("row", "col")),
        P(None, ("row", "col")),
    )
    return jax.shard_map(
        local, mesh=mesh, in_specs=placed, out_specs=(P(), P(None, ("row", "col"))), check_vma=False
    )
```

time: 972 us -> 178 us (0.18)
  waiting for transfers between devices: 773 us -> 0 us
  Pallas kernels: 0 us -> 166 us
  blocking collectives: 107 us -> 0 us
  other arithmetic: 36.2 us -> 7.34 us
  matrix products: 20.9 us -> 1.56 us
  local copies, waits for them, and re-layouts: 18.4 us -> 1.6 us
  between operations: 15.3 us -> 1.55 us
    psum x3 -> x0, waiting for transfers between devices: 566 us -> none  [local(): whole_sum = lax.psum(partial_rows, 'col')]
    all_gather x3 -> x0, waiting for transfers between devices: 206 us -> none  [local(): gathered = lax.all_gather(vector, 'row', axis=1, tiled=True)]
    pallas_call x0 -> x1, Pallas kernels: none -> 166 us  [local(): pl.pallas_call(kernel, out_shape=(jax.ShapeDtypeStruct((steps, 32, 128),...]
    psum x1 -> x0, blocking collectives: 107 us -> none  [local(): projections.append(reduce_mod(lax.psum(partial_terms, ('row', 'col'))))]
    dot_general x9 -> x0, matrix products: 19.3 us -> none  [the longest x3 10.6 us: local(): jnp.einsum('ntk,tdik->tdni', picked, a_digits, preferred_element_type=jnp...]
    select_n x7 -> x1, other arithmetic: 12.2 us -> 0.66 us  [local(): keys = jnp.where(index < tile_count[0, 0], tile_rows[0, 0], 32)]
    gather x3 -> x0, local copies, waits for them, and re-layouts: 11.2 us -> none  [local(): picked = jnp.take(v_digits, cols_here, axis=1)]
  transfers between devices with their start and end apart: 6 -> 0, of which waited for: 6 -> 0; matrix products, arithmetic and copies ran while one was open for 1% -> 0% of each run, Pallas kernels for 0% -> 0%
where the time goes in v1:
time: 178 us
  Pallas kernels  166 us (93%)
  other arithmetic  7.34 us (4%)
    pallas_call x1, Pallas kernels, local(): pl.pallas_call(kernel, out_shape=(jax.ShapeDtypeStruct((steps, 32, 128),...  166 us

profile of v1, /device:TPU:1, one launch (start us, length us, event | category | flops | bytes accessed | tf_op | source)
XLA Modules:
  0.0 178.0 jit_solution(740067459031358871)
XLA Ops:
  1.3 0.7 compare_select_fusion.72
  1.9 0.1 fusion.90
  2.1 0.1 convert_reduce_fusion.1
  2.2 0.6 pad_add_fusion.1.last_ref
  2.8 0.2 convert_reduce_fusion
  2.9 0.8 select_reduce_fusion.2
  3.7 0.1 compare_bitcast_fusion
  3.8 0.1 fusion.91
  3.9 0.6 pad_add_fusion.order_ref
  4.5 165.9 %shard_map.77 = (f32[3,32,128]{2,1,0:T(8,128)}, f32[64,256]{1,0:T(8,128)}) custom-call(s32[3,64]{1,0:T(4,128)} %pad_add_fusion.order_ref, s32[2,32]{1,0:T(2,128)} %pad_add_fusion.1.last_ref, f32[64,128,128]{2,1,0:T(8,128)} %bitcast.25, f32[64,256]{1,0:T(8,128)} %x_ref.1, f32[64,256]{1,0:T(8,128)} %y_ref.1), custom_call_target="tpu_custom_call" | custom-call | tf_op jit(solution)/shard_map/pallas_call | solution.py:373
  170.5 1.0 fusion.101
  171.4 1.5 broadcast_multiply_fusion
  173.0 0.2 convolution_bitcast_fusion
  173.2 0.2 fusion.80
  173.3 0.1 copy.16
  173.5 0.1 copy.17
  173.7 0.3 fusion.36
  174.0 0.4 fusion.18
  174.4 0.2 fusion.43
  174.7 0.2 fusion.35
  174.9 0.1 copy.19
  175.0 0.1 copy.20
  175.1 0.3 fusion.47
  175.4 0.4 fusion.17
  175.9 0.2 fusion.26
  176.1 0.3 fusion.22
  176.4 0.1 copy.22
  176.5 0.1 copy.23
  176.6 0.3 fusion.54
  177.0 0.3 multiply_floor_fusion
  177.3 0.7 fusion.23
  (24 shorter events, 0.4 us)

commit v2 on v1

--- a/solution.py
+++ b/solution.py
@@ -37,8 +37,8 @@
 
 def kernel(
     order_ref, last_ref, entries_ref, x_ref, y_ref, c_ref, v_ref,
-    ent, adig, xdig, gat, vdig, prods, part, lbuf, sbuf, ybuf, ysrc, vbuf, cloc, chalf, crecv, axb, ayb, azb,
-    ent_sem, ys, yr, xs, xr, rs, rr, bs, br, ls, lr, hs, hr, ps, pr, cs, cr, axs, axr, ays, ayr, azs, azr,
+    ent, adig, xdig, gat, vdig, prods, part, lbuf, sbuf, ybuf, ysrc, vbuf, xall, cloc, chalf, crecv, axb, ayb, azb, cfull,
+    ent_sem, ys, yr, xs, xr, rs, rr, bs, br, ls, lr, hs, hr, ps, pr, qs, qr, cs, cr, axs, axr, ays, ayr, azs, azr,
 ):
     row, col = lax.axis_index("row"), lax.axis_index("col")
     core, yl, px = row % 2, (row // 2) % NYL, row // (2 * NYL)
@@ -200,7 +200,7 @@
             total = times15(fold(sums[64:128])) + (fold(sums[0:64]) << 8) + sums[128:192]
             part[slot, :, j * 128 : (j + 1) * 128] = reduce_mod(fold(total).astype(F32))
 
-    def reduce(i):
+    def reduce(i, between):
         sends = []
 
         def long_copy(src, k, q):
@@ -220,132 +220,205 @@
             slot = slot_of(pz - 3 * step_r, q)
             fill(slot)
             start(short_copy(part.at[slot], 0, q))
+        for shift in (3, -2, 2, -1, 1, 0):
+            for q in range(2):
+                fill(slot_of(pz + shift * step_r, q))
+        between(0)
         for k in range(3):
             for q in range(2):
                 slot = slot_of(pz + (3 - k) * step_r, q)
-                fill(slot)
                 long_copy(part.at[slot], k, q).wait_recv()
                 lbuf[i, k, q] = lbuf[i, k, q] + part[slot]
                 start(long_copy(lbuf.at[i, k, q], k + 1, q))
                 if k < 2:
                     slot = slot_of(pz - (2 - k) * step_r, q)
-                    fill(slot)
                     short_copy(part.at[slot], k, q).wait_recv()
                     sbuf[i, k, q] = sbuf[i, k, q] + part[slot]
                     start(short_copy(sbuf.at[i, k, q], k + 1, q))
+            between(k + 1)
         swap = remote(ysrc.at[i], ybuf.at[i], ps.at[i], pr.at[i], dev_y(4))
         for q in range(2):
             slot = slot_of(pz, q)
-            fill(slot)
             short_copy(part.at[slot], 2, q).wait_recv()
             long_copy(part.at[slot], 3, q).wait_recv()
             whole = lbuf[i, 3, q] + sbuf[i, 2, q] + part[slot]
             if q == 0:
                 ysrc[i] = whole
                 swap.start()
+        between(4)
         swap.wait_recv()
         vbuf[i + 1] = reduce_mod(whole + ybuf[i])
-        for copy in sends:
-            copy.wait_send()
-        swap.wait_send()
-
-    def project(i):
-        high, low = split_digits(vbuf[i + 1])
-        digits = jnp.concatenate([high.astype(BF16), low.astype(BF16)], 0)
-        products = lax.dot_general(
-            xdig[...], digits, (((1,), (1,)), ((), ())), preferred_element_type=F32
+        sends.append(swap)
+        return sends
+
+    left_half = lax.broadcasted_iota(I32, (64, 128), 1) < 64
+
+    def quads(products):
+        upper, lower = products[0:64], pltpu.roll(products[64:128], 64, 1)
+        mixed = jnp.where(left_half, times15(fold(upper)) + lower, fold(upper + lower) << 8)
+        return reduce_mod(fold(mixed + pltpu.roll(mixed, 64, 1)).astype(F32))
+
+    def stacked(values):
+        high, low = split_digits(values)
+        return jnp.concatenate([high.astype(BF16), low.astype(BF16)], 0)
+
+    def project(x_digits, values):
+        return lax.dot_general(
+            x_digits, stacked(values), (((1,), (1,)), ((), ())), preferred_element_type=F32
         ).astype(I32)
-        upper, lower = products[0:64], pltpu.roll(products[64:128], 64, 1)
-        left_half = lax.broadcasted_iota(I32, (64, 128), 1) < 64
-        mixed = jnp.where(left_half, times15(fold(upper)) + lower, fold(upper + lower) << 8)
-        residues = reduce_mod(fold(mixed + pltpu.roll(mixed, 64, 1)).astype(F32))
+
+    def keep_terms(i, products):
+        residues = quads(products)
         cloc[i] = jnp.where(left_half[0:32], residues[0:32], residues[32:64])
+
+    mine = pl.ds(16 * core, 16)
+    theirs = pl.ds(16 - 16 * core, 16)
+    pending = []
+
+    def sum_stages(i):
+        first = remote(cloc.at[i, theirs], crecv.at[i], cs.at[i, 0], cr.at[i, 0], sibling)
+        last = remote(chalf.at[i, 3], cfull.at[i, mine], cs.at[i, 1], cr.at[i, 1], sibling)
+
+        def copies(k, count, landing, ssem, rsem, dev):
+            return [
+                remote(chalf.at[i, k], landing.at[i, d - 1], ssem.at[i, d - 1], rsem.at[i, d - 1], dev(d))
+                for d in range(1, count)
+            ]
+
+        rounds = [
+            (copies(0, NX, axb, axs, axr, dev_x), axb),
+            (copies(1, NYL * NYH, ayb, ays, ayr, dev_y), ayb),
+            (copies(2, NZ, azb, azs, azr, dev_z), azb),
+        ]
+
+        def begin(k):
+            for copy in rounds[k][0]:
+                copy.start()
+            pending.extend(rounds[k][0])
+
+        def finish(k):
+            total = chalf[i, k]
+            for d, copy in enumerate(rounds[k][0]):
+                copy.wait_recv()
+                total = total + rounds[k][1][i, d]
+            chalf[i, k + 1] = total if k == 0 else reduce_mod(total)
+
+        def stage(n):
+            if n == 0:
+                first.start()
+                pending.append(first)
+            elif n == 1:
+                first.wait_recv()
+                chalf[i, 0] = cloc[i, mine] + crecv[i]
+                begin(0)
+            elif n < 4:
+                finish(n - 2)
+                begin(n - 1)
+            elif n == 4:
+                finish(2)
+                last.start()
+                pending.append(last)
+                cfull[i, mine] = chalf[i, 3]
+            else:
+                last.wait_recv()
+
+        return stage
+
+    def twice(i):
+        packed = cfull[i]
+        turned = pltpu.roll(packed, 64, 1)
+        return jnp.concatenate(
+            [jnp.where(left_half[0:32], packed, turned), jnp.where(left_half[0:32], turned, packed)], 0
+        )
+
+    def times(left, right):
+        left_digits = stacked(left)[:, 0:64]
+        high, low = split_digits(right)
+        right_digits = jnp.where(left_half, high, low).astype(BF16)
+        return quads(jnp.dot(left_digits, right_digits, preferred_element_type=F32).astype(I32))
+
+    def send_x(source, where, k):
+        copies = []
+        for d in range(1, NZ):
+            copies.append(remote(source, xall.at[where], qs.at[k, d], qr.at[k, d], dev_z(d)))
+            copies[-1].start()
+        pending.extend(copies)
+
+    partner_col = (1 - yh) * NZ + pz
+    x_swap = remote(x_ref, xall.at[col], qs.at[0, 0], qr.at[0, 0], dev_y(4))
+    x_swap.start()
+    pending.append(x_swap)
+    send_x(x_ref, col, 0)
+    xall[col] = x_ref[...]
+
+    stages = [sum_stages(i) for i in range(STEP_COUNT)]
 
     gather(0, first_between)
     multiply(0)
-    reduce(0)
-    project(0)
-
-    def later(i, carry):
-        gather(i, nothing)
-        multiply(i)
-        reduce(i)
-        project(i)
-        return carry
-
-    lax.fori_loop(1, STEP_COUNT, later, 0)
-    v_ref[...] = vbuf[STEP_COUNT]
-
-    halves = [remote(cloc.at[:, pl.ds(16 * (1 - core), 16)], crecv, cs.at[0], cr.at[0], sibling)]
-    halves[0].start()
-    halves[0].wait_recv()
-    chalf[0] = cloc[:, pl.ds(16 * core, 16)] + crecv[...]
-
-    def exchange(k, count, landing, ssem, rsem, dev):
-        copies = []
-        for d in range(1, count):
-            copies.append(remote(chalf.at[k], landing.at[d - 1], ssem.at[d - 1], rsem.at[d - 1], dev(d)))
-            copies[-1].start()
-        total = chalf[k]
-        for d in range(1, count):
-            copies[d - 1].wait_recv()
-            total = total + landing[d - 1]
-        chalf[k + 1] = total if k == 0 else reduce_mod(total)
-        halves.extend(copies)
-
-    exchange(0, NX, axb, axs, axr, dev_x)
-    exchange(1, NYL * NYH, ayb, ays, ayr, dev_y)
-    exchange(2, NZ, azb, azs, azr, dev_z)
-    mine = pl.ds(16 * core, 16)
-    swap = remote(chalf.at[3], c_ref.at[:, mine], cs.at[1], cr.at[1], sibling)
-    swap.start()
-    c_ref[:, mine] = chalf[3]
-    swap.wait_recv()
-    swap.wait_send()
-    for copy in halves:
+    sends = reduce(0, nothing)
+    remote(x_ref, xall.at[partner_col], qs.at[0, 0], qr.at[0, 0], dev_y(4)).wait_recv()
+
+    def second_between(stage):
+        if stage == 0:
+            send_x(xall.at[partner_col], partner_col, 1)
+            keep_terms(0, project(xdig[...], vbuf[1]))
+        stages[0](stage)
+
+    def second_reduce(stage):
+        if stage == 0:
+            stages[0](4)
+        if stage == 1:
+            stages[0](5)
+
+    gather(1, second_between)
+    multiply(1)
+    for copy in sends:
         copy.wait_send()
-
-
-def combine_parts(high_part, middle_part, low_part):
-    return reduce_mod(
-        15.0 * reduce_mod(high_part)
-        + reduce_mod(256.0 * reduce_mod(middle_part))
-        + reduce_mod(low_part)
-    )
-
-
-def poly_product(left_side, right_side):
-    span_width = left_side.shape[-1]
-    left_high, left_low = split_digits(left_side)
-    right_high, right_low = split_digits(right_side)
-    stacked_left = jnp.concatenate([left_high, left_low], 1).astype(BF16)
-    stacked_right = jnp.concatenate([right_high, right_low], 2).astype(BF16)
-    products = jnp.einsum("kmj,kjn->kmn", stacked_left, stacked_right, preferred_element_type=F32)
-    return combine_parts(
-        products[:, :span_width, :span_width],
-        products[:, :span_width, span_width:] + products[:, span_width:, :span_width],
-        products[:, span_width:, span_width:],
-    )
-
-
-def sigma_update(projections):
-    span_width = projections[0].shape[0]
-    term_count = len(projections) + 1
-    identity = jnp.eye(span_width, dtype=F32)[None]
-    polynomial = jnp.concatenate(
-        [identity, jnp.zeros((term_count - 1, span_width, span_width), F32)], 0
-    )
-    for step_index in range(1, term_count):
-        known_terms = jnp.stack(
-            [projections[step_index - 1 - shift] for shift in range(step_index)]
-        )
-        discrepancy = reduce_mod(jnp.sum(poly_product(polynomial[:step_index], known_terms), 0))
-        scaled = poly_product(jnp.broadcast_to(discrepancy, polynomial.shape), polynomial)
-        shifted = jnp.concatenate(
-            [jnp.zeros((1, span_width, span_width), F32), polynomial[:-1]], 0
-        )
-        polynomial = reduce_mod(shifted - scaled)
-    return polynomial
+    sends = reduce(1, second_reduce)
+
+    def third_between(stage):
+        if stage == 0:
+            keep_terms(1, project(xdig[...], vbuf[2]))
+        stages[1](stage)
+
+    gather(2, third_between)
+    stages[1](4)
+    multiply(2)
+    stages[1](5)
+    for copy in sends:
+        copy.wait_send()
+    for k in range(2):
+        for d in range(1, NZ):
+            where = (yh if k == 0 else 1 - yh) * NZ + (pz - d + NZ) % NZ
+            remote(x_ref, xall.at[where], qs.at[k, d], qr.at[k, d], dev_z(d)).wait_recv()
+
+    known = {}
+
+    def third_reduce(stage):
+        if stage == 0:
+            total = jnp.zeros((128, 128), I32)
+            for slot in range(16):
+                total = total + project(stacked(xall[slot]), part[slot])
+            keep_terms(2, total)
+            stages[2](0)
+            first, second = twice(0), twice(1)
+            known["zero"] = reduce_mod(-first)
+            error = reduce_mod(times(known["zero"], second) + first)
+            known["one"] = reduce_mod(known["zero"] - error)
+            known["zero"] = reduce_mod(-times(error, known["zero"]))
+            known["rest"] = times(known["one"], second) + first
+            stages[2](1)
+        else:
+            stages[2](stage + 1)
+
+    sends = reduce(2, third_reduce)
+    v_ref[...] = vbuf[STEP_COUNT] / MODULUS
+    error = reduce_mod(times(known["zero"], twice(2)) + known["rest"])
+    c_ref[0] = (reduce_mod(-times(error, known["zero"])) / MODULUS)[:, 0:64]
+    c_ref[1] = (reduce_mod(known["zero"] - times(error, known["one"])) / MODULUS)[:, 0:64]
+    c_ref[2] = (reduce_mod(known["one"] - error) / MODULUS)[:, 0:64]
+    for copy in sends + pending:
+        copy.wait_send()
 
 
 def local(tile_entries, tile_rows, tile_cols, tile_count, block_x, block_y):
@@ -370,10 +443,10 @@
     smem = pl.BlockSpec(memory_space=pltpu.SMEM)
     steps = STEP_COUNT
     dma = pltpu.SemaphoreType.DMA
-    projections, vector = pl.pallas_call(
+    return pl.pallas_call(
         kernel,
         out_shape=(
-            jax.ShapeDtypeStruct((steps, 32, 128), F32),
+            jax.ShapeDtypeStruct((steps, 64, 64), F32),
             jax.ShapeDtypeStruct((64, 256), F32),
         ),
         in_specs=[smem, smem, pl.BlockSpec(memory_space=pl.ANY), vmem, vmem],
@@ -391,12 +464,14 @@
             pltpu.VMEM((steps, 64, 256), F32),
             pltpu.VMEM((steps, 64, 256), F32),
             pltpu.VMEM((steps + 1, 64, 256), F32),
+            pltpu.VMEM((16, 64, 256), F32),
             pltpu.VMEM((steps, 32, 128), F32),
-            pltpu.VMEM((4, steps, 16, 128), F32),
+            pltpu.VMEM((steps, 4, 16, 128), F32),
             pltpu.VMEM((steps, 16, 128), F32),
-            pltpu.VMEM((NX - 1, steps, 16, 128), F32),
-            pltpu.VMEM((7, steps, 16, 128), F32),
-            pltpu.VMEM((7, steps, 16, 128), F32),
+            pltpu.VMEM((steps, NX - 1, 16, 128), F32),
+            pltpu.VMEM((steps, 7, 16, 128), F32),
+            pltpu.VMEM((steps, 7, 16, 128), F32),
+            pltpu.VMEM((steps, 32, 128), F32),
             dma((8,)),
             dma((steps, 3)), dma((steps, 3)),
             dma((steps, 4, 2)), dma((steps, 4, 2)),
@@ -405,18 +480,16 @@
             dma((steps, 4, 2)), dma((steps, 4, 2)),
             dma((steps, 3, 2)), dma((steps, 3, 2)),
             dma((steps,)), dma((steps,)),
-            dma((2,)), dma((2,)),
-            dma((3,)), dma((3,)),
-            dma((7,)), dma((7,)),
-            dma((7,)), dma((7,)),
+            dma((2, 8)), dma((2, 8)),
+            dma((steps, 2)), dma((steps, 2)),
+            dma((steps, 3)), dma((steps, 3)),
+            dma((steps, 7)), dma((steps, 7)),
+            dma((steps, 7)), dma((steps, 7)),
         ],
         compiler_params=pltpu.CompilerParams(
             collective_id=0, has_side_effects=True, vmem_limit_bytes=56 * 1024 * 1024
         ),
     )(order_table, last_table, entries, block_x, block_y)
-    projections = jnp.concatenate([projections[:, :, :64], projections[:, :, 64:]], 1)
-    polynomial = sigma_update([projections[n] for n in range(steps)])
-    return (polynomial[:-1] / MODULUS, vector / MODULUS)
 
 
 def solution(mesh):

time: 178 us -> 163 us (0.916)
  Pallas kernels: 166 us -> 154 us
  other arithmetic: 7.34 us -> 3.21 us
    pallas_call x1, Pallas kernels: 166 us -> 154 us  [local(): pl.pallas_call(kernel, out_shape=(jax.ShapeDtypeStruct((steps, 64, 64), F...]
    unnamed x0 -> x2, local copies, waits for them, and re-layouts: none -> 3.01 us
    div x2 -> x0, other arithmetic: 2.16 us -> none  [local(): return (polynomial[:-1] / MODULUS, vector / MODULUS)]
where the time goes in v2:
time: 163 us; the launch traced here: 162 us
  Pallas kernels  154 us (94%)
  other arithmetic  3.21 us (2%)
  local copies, waits for them, and re-layouts  3.01 us (2%)
    pallas_call x1, Pallas kernels, local(): pl.pallas_call(kernel, out_shape=(jax.ShapeDtypeStruct((steps, 64, 64), F...  154 us

profile of v2, /device:TPU:1, one launch (start us, length us, event | category | flops | bytes accessed | tf_op | source)
XLA Modules:
  0.0 161.7 jit_solution(131428038273223611)
XLA Ops:
  1.3 0.7 compare_select_fusion
  1.9 0.1 fusion.2
  2.1 0.1 convert_reduce_fusion.1
  2.2 0.6 pad_add_fusion.1.last_ref
  2.8 0.2 convert_reduce_fusion
  2.9 0.8 select_reduce_fusion.2
  3.7 0.1 compare_bitcast_fusion
  3.8 0.1 fusion.3
  3.9 0.6 pad_add_fusion.order_ref
  4.5 154.2 %shard_map.77 = (f32[3,64,64]{2,1,0:T(8,128)}, f32[64,256]{1,0:T(8,128)}) custom-call(s32[3,64]{1,0:T(4,128)} %pad_add_fusion.order_ref, s32[2,32]{1,0:T(2,128)} %pad_add_fusion.1.last_ref, f32[64,128,128]{2,1,0:T(8,128)} %bitcast.14, f32[64,256]{1,0:T(8,128)} %x_ref.1, f32[64,256]{1,0:T(8,128)} %y_ref.1), custom_call_target="tpu_custom_call" | custom-call | tf_op jit(solution)/shard_map/pallas_call | solution.py:446
  158.7 1.5 copy.11
  160.2 1.5 copy.12
  (1 shorter events, 0.0 us)

commit v3 on v2

--- a/solution.py
+++ b/solution.py
@@ -12,6 +12,7 @@
 INVERSE = 1.0 / 65521.0
 MESH = pl.DeviceIdType.MESH
 NX, NYL, NYH, NZ = 4, 4, 2, 8
+DIRECT = (0, 1, 2, 3)
 F32, I32, BF16 = jnp.float32, jnp.int32, jnp.bfloat16
 
 
@@ -36,9 +37,9 @@
 
 
 def kernel(
-    order_ref, last_ref, entries_ref, x_ref, y_ref, c_ref, v_ref,
-    ent, adig, xdig, gat, vdig, prods, part, lbuf, sbuf, ybuf, ysrc, vbuf, xall, cloc, chalf, crecv, axb, ayb, azb, cfull,
-    ent_sem, ys, yr, xs, xr, rs, rr, bs, br, ls, lr, hs, hr, ps, pr, qs, qr, cs, cr, axs, axr, ays, ayr, azs, azr,
+    rows_ref, cols_ref, count_ref, entries_ref, x_ref, y_ref, c_ref, v_ref,
+    ent, adig, xdig, gat, vdig, prods, part, lbuf, sbuf, ybuf, ysrc, vbuf, xall, cloc, chalf, crecv, axb, ayb, azb, cfull, xall_digits, tables, table,
+    table_sem, ent_sem, ys, yr, xs, xr, rs, rr, bs, br, ls, lr, hs, hr, ps, pr, qs, qr, cs, cr, axs, axr, ays, ayr, azs, azr,
 ):
     row, col = lax.axis_index("row"), lax.axis_index("col")
     core, yl, px = row % 2, (row // 2) % NYL, row // (2 * NYL)
@@ -105,6 +106,8 @@
         def both_x(src, r, d):
             send(src, piece(r), xs.at[i, d, 0], xr.at[i, d, 0], dev_x(1))
             send(src, piece(r), xs.at[i, d, 1], xr.at[i, d, 1], dev_x(-1))
+            if d in DIRECT:
+                send(src, piece(r), rs.at[i, d], rr.at[i, d], dev_x(2))
 
         def to_sibling(src, r, n):
             send(src, piece(r), bs.at[i, n], br.at[i, n], sibling)
@@ -120,7 +123,8 @@
         def relay(d):
             near = rid(px - step_r, yl - d, core)
             arrive(near, xr.at[i, d, core])
-            send(piece(near), piece(near), rs.at[i, d], rr.at[i, d], dev_x(step_r))
+            if d not in DIRECT:
+                send(piece(near), piece(near), rs.at[i, d], rr.at[i, d], dev_x(step_r))
             to_sibling(piece(near), near, 4 + d)
 
         for d in range(1, NYL):
@@ -144,17 +148,47 @@
         for copy in sends:
             copy.wait_send()
 
+    def make_tables():
+        shape = (tile_total, tile_total)
+        down, across = lax.broadcasted_iota(I32, shape, 0), lax.broadcasted_iota(I32, shape, 1)
+
+        def upright(flat):
+            return jnp.sum(jnp.where(down == across, flat, 0), 1, keepdims=True)
+
+        def add_up(values):
+            return jnp.sum(values, 0, keepdims=True)
+
+        tables[...] = jnp.zeros((8, 128), I32)
+        live = across < count_ref[0, 0]
+        flat_keys = jnp.where(live, jnp.broadcast_to(rows_ref[...], shape), 32)
+        keys = upright(flat_keys)
+        earlier = (flat_keys == keys) & (across < down)
+        rank = jnp.sum(((flat_keys < keys) | earlier).astype(I32), 1, keepdims=True)
+        repeated = jnp.max(earlier.astype(I32), 1, keepdims=True)
+        chosen = rank == across
+        columns = upright(jnp.broadcast_to(cols_ref[...], shape))
+        tables[0:1, 0:64] = add_up(jnp.where(chosen, down, 0))
+        tables[1:2, 0:64] = add_up(jnp.where(chosen, columns, 0))
+        tables[2:3, 0:64] = add_up(jnp.where(chosen, -repeated, 0))
+        tables[3:4, 0:64] = jnp.maximum(add_up((keys <= across).astype(I32)) - 1, 0)
+        tables[4:5, 0:64] = -jnp.max((keys == across).astype(I32), 0, keepdims=True)
+        return pltpu.make_async_copy(tables, table, table_sem)
+
     def make_digits(n):
         @pl.loop(n * chunk, (n + 1) * chunk)
         def _(t):
             high, low = split_digits(ent[t].T)
-            adig[t, 0:128, :] = high.astype(BF16)
-            adig[t, 128:256, :] = low.astype(BF16)
+            adig[t, :, 0:128] = high.astype(BF16)
+            adig[t, :, 128:256] = low.astype(BF16)
 
     def nothing(stage):
         del stage
 
     def first_between(stage):
+        if stage == 0:
+            moved = make_tables()
+            moved.start()
+            moved.wait()
         for n in (2 * stage, 2 * stage + 1):
             entry_copy(n).wait()
             make_digits(n)
@@ -167,24 +201,15 @@
                 vdig[2 * r + j, 0:64, :] = high[:, j * 128 : (j + 1) * 128].astype(BF16)
                 vdig[2 * r + j, 64:128, :] = low[:, j * 128 : (j + 1) * 128].astype(BF16)
 
-        blank = jnp.zeros((64, 128), BF16)
-        width = 4
+        width = 16
 
         def body(n, total):
             for u in range(width):
                 j = n * width + u
-                digits = vdig[order_ref[1, j]]
-                high, low = digits[0:64], digits[64:128]
-                left = jnp.concatenate(
-                    [
-                        jnp.concatenate([low, high], 1),
-                        jnp.concatenate([high, blank], 1),
-                        jnp.concatenate([blank, low], 1),
-                    ],
-                    0,
-                )
-                product = jnp.dot(left, adig[order_ref[0, j]], preferred_element_type=F32)
-                total = (total & order_ref[2, j]) + product.astype(I32)
+                p = jnp.dot(vdig[table[1, j]], adig[table[0, j]], preferred_element_type=F32)
+                middle = p[0:64, 128:256] + p[64:128, 0:128]
+                product = jnp.concatenate([middle, p[0:64, 0:128], p[64:128, 128:256]], 0)
+                total = (total & table[2, j]) + product.astype(I32)
                 prods[j] = total
             return total
 
@@ -196,7 +221,7 @@
     def fill(slot):
         for j in range(2):
             b = 2 * slot + j
-            sums = prods[last_ref[0, b]] & last_ref[1, b]
+            sums = prods[table[3, b]] & table[4, b]
             total = times15(fold(sums[64:128])) + (fold(sums[0:64]) << 8) + sums[128:192]
             part[slot, :, j * 128 : (j + 1) * 128] = reduce_mod(fold(total).astype(F32))
 
@@ -213,42 +238,50 @@
             copy.start()
             sends.append(copy)
 
-        for q in range(2):
-            slot = slot_of(pz + 4, q)
-            fill(slot)
-            start(long_copy(part.at[slot], 0, q))
-            slot = slot_of(pz - 3 * step_r, q)
-            fill(slot)
-            start(short_copy(part.at[slot], 0, q))
+        def own(z, q):
+            return part.at[slot_of(z, q // 2), pl.ds(32 * (q % 2), 32)]
+
+        for q in range(4):
+            if q % 2 == 0:
+                fill(slot_of(pz + 4, q // 2))
+            start(long_copy(own(pz + 4, q), 0, q))
+            if q % 2 == 0:
+                fill(slot_of(pz - 3 * step_r, q // 2))
+            start(short_copy(own(pz - 3 * step_r, q), 0, q))
         for shift in (3, -2, 2, -1, 1, 0):
             for q in range(2):
                 fill(slot_of(pz + shift * step_r, q))
         between(0)
         for k in range(3):
-            for q in range(2):
-                slot = slot_of(pz + (3 - k) * step_r, q)
-                long_copy(part.at[slot], k, q).wait_recv()
-                lbuf[i, k, q] = lbuf[i, k, q] + part[slot]
+            for q in range(4):
+                mine_here = own(pz + (3 - k) * step_r, q)
+                long_copy(mine_here, k, q).wait_recv()
+                lbuf[i, k, q] = lbuf[i, k, q] + mine_here[...]
                 start(long_copy(lbuf.at[i, k, q], k + 1, q))
                 if k < 2:
-                    slot = slot_of(pz - (2 - k) * step_r, q)
-                    short_copy(part.at[slot], k, q).wait_recv()
-                    sbuf[i, k, q] = sbuf[i, k, q] + part[slot]
+                    mine_here = own(pz - (2 - k) * step_r, q)
+                    short_copy(mine_here, k, q).wait_recv()
+                    sbuf[i, k, q] = sbuf[i, k, q] + mine_here[...]
                     start(short_copy(sbuf.at[i, k, q], k + 1, q))
             between(k + 1)
-        swap = remote(ysrc.at[i], ybuf.at[i], ps.at[i], pr.at[i], dev_y(4))
+        swaps = []
+        wholes = []
+        for q in range(4):
+            mine_here = own(pz, q)
+            short_copy(mine_here, 2, q).wait_recv()
+            long_copy(mine_here, 3, q).wait_recv()
+            whole = lbuf[i, 3, q] + sbuf[i, 2, q] + mine_here[...]
+            if q < 2:
+                ysrc[i, q] = whole
+                swaps.append(remote(ysrc.at[i, q], ybuf.at[i, q], ps.at[i, q], pr.at[i, q], dev_y(4)))
+                swaps[-1].start()
+            else:
+                wholes.append(whole)
+        between(4)
         for q in range(2):
-            slot = slot_of(pz, q)
-            short_copy(part.at[slot], 2, q).wait_recv()
-            long_copy(part.at[slot], 3, q).wait_recv()
-            whole = lbuf[i, 3, q] + sbuf[i, 2, q] + part[slot]
-            if q == 0:
-                ysrc[i] = whole
-                swap.start()
-        between(4)
-        swap.wait_recv()
-        vbuf[i + 1] = reduce_mod(whole + ybuf[i])
-        sends.append(swap)
+            swaps[q].wait_recv()
+            vbuf[i + 1, pl.ds(32 * q, 32)] = reduce_mod(wholes[q] + ybuf[i, q])
+        sends.extend(swaps)
         return sends
 
     left_half = lax.broadcasted_iota(I32, (64, 128), 1) < 64
@@ -376,9 +409,18 @@
         copy.wait_send()
     sends = reduce(1, second_reduce)
 
+    def receive_x():
+        for k in range(2):
+            for d in range(1, NZ):
+                where = (yh if k == 0 else 1 - yh) * NZ + (pz - d + NZ) % NZ
+                remote(x_ref, xall.at[where], qs.at[k, d], qr.at[k, d], dev_z(d)).wait_recv()
+
     def third_between(stage):
         if stage == 0:
             keep_terms(1, project(xdig[...], vbuf[2]))
+            receive_x()
+        for slot in range(4 * stage, 4 * stage + 4):
+            xall_digits[slot] = stacked(xall[slot])
         stages[1](stage)
 
     gather(2, third_between)
@@ -387,18 +429,13 @@
     stages[1](5)
     for copy in sends:
         copy.wait_send()
-    for k in range(2):
-        for d in range(1, NZ):
-            where = (yh if k == 0 else 1 - yh) * NZ + (pz - d + NZ) % NZ
-            remote(x_ref, xall.at[where], qs.at[k, d], qr.at[k, d], dev_z(d)).wait_recv()
-
     known = {}
 
     def third_reduce(stage):
         if stage == 0:
             total = jnp.zeros((128, 128), I32)
             for slot in range(16):
-                total = total + project(stacked(xall[slot]), part[slot])
+                total = total + project(xall_digits[slot], part[slot])
             keep_terms(2, total)
             stages[2](0)
             first, second = twice(0), twice(1)
@@ -424,21 +461,6 @@
 def local(tile_entries, tile_rows, tile_cols, tile_count, block_x, block_y):
     entries = tile_entries[0, 0]
     slots = entries.shape[0]
-    index = jnp.arange(slots, dtype=I32)
-    keys = jnp.where(index < tile_count[0, 0], tile_rows[0, 0], 32)
-    before = (keys[None, :] < keys[:, None]) | ((keys[None, :] == keys[:, None]) & (index[None, :] < index[:, None]))
-    rank = jnp.sum(before.astype(I32), 1)
-    chosen = (rank[None, :] == index[:, None]).astype(I32)
-    order = jnp.sum(chosen * index[None, :], 1)
-    columns = jnp.sum(chosen * tile_cols[0, 0][None, :], 1)
-    sorted_keys = jnp.sum(chosen * keys[None, :], 1)
-    same = jnp.concatenate([jnp.zeros((1,), jnp.bool_), sorted_keys[1:] == sorted_keys[:-1]])
-    order_table = jnp.stack([order, columns, -same.astype(I32)])
-    blocks = jnp.arange(32, dtype=I32)
-    below = jnp.sum((keys[None, :] <= blocks[:, None]).astype(I32), 1)
-    found = jnp.any(keys[None, :] == blocks[:, None], 1)
-    last_table = jnp.stack([jnp.maximum(below - 1, 0), -found.astype(I32)])
-
     vmem = pl.BlockSpec(memory_space=pltpu.VMEM)
     smem = pl.BlockSpec(memory_space=pltpu.SMEM)
     steps = STEP_COUNT
@@ -449,20 +471,20 @@
             jax.ShapeDtypeStruct((steps, 64, 64), F32),
             jax.ShapeDtypeStruct((64, 256), F32),
         ),
-        in_specs=[smem, smem, pl.BlockSpec(memory_space=pl.ANY), vmem, vmem],
+        in_specs=[vmem, vmem, smem, pl.BlockSpec(memory_space=pl.ANY), vmem, vmem],
         out_specs=(vmem, vmem),
         scratch_shapes=[
             pltpu.VMEM((slots, 128, 128), F32),
-            pltpu.VMEM((slots, 256, 128), BF16),
+            pltpu.VMEM((slots, 128, 256), BF16),
             pltpu.VMEM((128, 256), BF16),
             pltpu.VMEM((steps, 32, 64, 256), F32),
             pltpu.VMEM((64, 128, 128), BF16),
             pltpu.VMEM((slots, 192, 128), I32),
             pltpu.VMEM((16, 64, 256), F32),
-            pltpu.VMEM((steps, 4, 2, 64, 256), F32),
-            pltpu.VMEM((steps, 3, 2, 64, 256), F32),
-            pltpu.VMEM((steps, 64, 256), F32),
-            pltpu.VMEM((steps, 64, 256), F32),
+            pltpu.VMEM((steps, 4, 4, 32, 256), F32),
+            pltpu.VMEM((steps, 3, 4, 32, 256), F32),
+            pltpu.VMEM((steps, 2, 32, 256), F32),
+            pltpu.VMEM((steps, 2, 32, 256), F32),
             pltpu.VMEM((steps + 1, 64, 256), F32),
             pltpu.VMEM((16, 64, 256), F32),
             pltpu.VMEM((steps, 32, 128), F32),
@@ -472,14 +494,18 @@
             pltpu.VMEM((steps, 7, 16, 128), F32),
             pltpu.VMEM((steps, 7, 16, 128), F32),
             pltpu.VMEM((steps, 32, 128), F32),
+            pltpu.VMEM((16, 128, 256), BF16),
+            pltpu.VMEM((8, 128), I32),
+            pltpu.SMEM((8, 128), I32),
+            dma(()),
             dma((8,)),
             dma((steps, 3)), dma((steps, 3)),
             dma((steps, 4, 2)), dma((steps, 4, 2)),
             dma((steps, 4)), dma((steps, 4)),
             dma((steps, 16)), dma((steps, 16)),
-            dma((steps, 4, 2)), dma((steps, 4, 2)),
-            dma((steps, 3, 2)), dma((steps, 3, 2)),
-            dma((steps,)), dma((steps,)),
+            dma((steps, 4, 4)), dma((steps, 4, 4)),
+            dma((steps, 3, 4)), dma((steps, 3, 4)),
+            dma((steps, 2)), dma((steps, 2)),
             dma((2, 8)), dma((2, 8)),
             dma((steps, 2)), dma((steps, 2)),
             dma((steps, 3)), dma((steps, 3)),
@@ -489,7 +515,7 @@
         compiler_params=pltpu.CompilerParams(
             collective_id=0, has_side_effects=True, vmem_limit_bytes=56 * 1024 * 1024
         ),
-    )(order_table, last_table, entries, block_x, block_y)
+    )(tile_rows[0], tile_cols[0], tile_count, entries, block_x, block_y)
 
 
 def solution(mesh):

time: 163 us -> 147 us (0.902)
  Pallas kernels: 154 us -> 141 us
  other arithmetic: 3.21 us -> 0 us
    pallas_call x1, Pallas kernels: 154 us -> 141 us  [local(): pl.pallas_call(kernel, out_shape=(jax.ShapeDtypeStruct((steps, 64, 64), F...]
where the time goes in v3:
time: 147 us; the launch traced here: 145 us
  Pallas kernels  141 us (96%)
  local copies, waits for them, and re-layouts  3.01 us (2%)
    pallas_call x1, Pallas kernels, local(): pl.pallas_call(kernel, out_shape=(jax.ShapeDtypeStruct((steps, 64, 64), F...  141 us
    unnamed x2, local copies, waits for them, and re-layouts  3.01 us

profile of v3, /device:TPU:1, one launch (start us, length us, event | category | flops | bytes accessed | tf_op | source)
XLA Modules:
  0.0 145.3 jit_solution(14407750700249954349)
XLA Ops:
  1.3 141.0 %shard_map.77 = (f32[3,64,64]{2,1,0:T(8,128)}, f32[64,256]{1,0:T(8,128)}) custom-call(s32[1,64]{1,0:T(1,128)} %bitcast.4, s32[1,64]{1,0:T(1,128)} %bitcast.5, s32[1,1]{1,0:T(1,128)S(6)} %copy.10.count_ref, f32[64,128,128]{2,1,0:T(8,128)} %bitcast.3, f32[64,256]{1,0:T(8,128)} %x_ref.1, f32[64,256]{1,0:T(8,128)} %y_ref.1), custom_call_target="tpu_custom_call" | custom-call | tf_op jit(solution)/shard_map/pallas_call | solution.py:468
  142.3 1.5 %copy.11 = f32[3,64,64]{2,1,0:T(8,128)} copy(f32[3,64,64]{2,1,0:T(8,128)} %get-tuple-element.4) | data formatting | bytes 98304
  143.9 1.5 %copy.12 = f32[64,256]{1,0:T(8,128)} copy(f32[64,256]{1,0:T(8,128)} %get-tuple-element.5) | data formatting | bytes 131072

commit v4 on v3

--- a/solution.py
+++ b/solution.py
@@ -201,7 +201,7 @@
                 vdig[2 * r + j, 0:64, :] = high[:, j * 128 : (j + 1) * 128].astype(BF16)
                 vdig[2 * r + j, 64:128, :] = low[:, j * 128 : (j + 1) * 128].astype(BF16)
 
-        width = 16
+        width = 32
 
         def body(n, total):
             for u in range(width):
@@ -223,7 +223,8 @@
             b = 2 * slot + j
             sums = prods[table[3, b]] & table[4, b]
             total = times15(fold(sums[64:128])) + (fold(sums[0:64]) << 8) + sums[128:192]
-            part[slot, :, j * 128 : (j + 1) * 128] = reduce_mod(fold(total).astype(F32))
+            rest = fold(total).astype(F32)
+            part[slot, :, j * 128 : (j + 1) * 128] = rest - jnp.floor(rest * INVERSE) * MODULUS
 
     def reduce(i, between):
         sends = []

time: 147 us -> 146 us (level)
  no operation moved by 1% of the time
where the time goes in v4:
time: 146 us; the launch traced here: 144 us
  Pallas kernels  140 us (96%)
  local copies, waits for them, and re-layouts  3.01 us (2%)
    pallas_call x1, Pallas kernels, local(): pl.pallas_call(kernel, out_shape=(jax.ShapeDtypeStruct((steps, 64, 64), F...  140 us
    unnamed x2, local copies, waits for them, and re-layouts  3.01 us

profile of v4, /device:TPU:1, one launch (start us, length us, event | category | flops | bytes accessed | tf_op | source)
XLA Modules:
  0.0 144.2 jit_solution(11462447051613487039)
XLA Ops:
  1.3 139.9 %shard_map.77 = (f32[3,64,64]{2,1,0:T(8,128)}, f32[64,256]{1,0:T(8,128)}) custom-call(s32[1,64]{1,0:T(1,128)} %bitcast.4, s32[1,64]{1,0:T(1,128)} %bitcast.5, s32[1,1]{1,0:T(1,128)S(6)} %copy.10.count_ref, f32[64,128,128]{2,1,0:T(8,128)} %bitcast.3, f32[64,256]{1,0:T(8,128)} %x_ref.1, f32[64,256]{1,0:T(8,128)} %y_ref.1), custom_call_target="tpu_custom_call" | custom-call | tf_op jit(solution)/shard_map/pallas_call | solution.py:469
  141.2 1.5 %copy.11 = f32[3,64,64]{2,1,0:T(8,128)} copy(f32[3,64,64]{2,1,0:T(8,128)} %get-tuple-element.4) | data formatting | bytes 98304
  142.8 1.5 %copy.12 = f32[64,256]{1,0:T(8,128)} copy(f32[64,256]{1,0:T(8,128)} %get-tuple-element.5) | data formatting | bytes 131072
